TPU v7x, 32 devices: a whole 2x2x4 slice. The times are simulated.
32 devices in a mesh: row: 2 (over y), col: 16 (over z, x, core).
Axes of the slice: x: 2, y: 2, z: 4, core: 2. Of those that a mesh axis runs over, the one named last changes fastest.
Arguments:
- eigen_slab: float32 [2048, 16384], P('row', 'col'), may hold values from -6 to 6
- secular_poles: float32 [32768], P('col'), may hold values from 0 to 4, as said below
- coupling: float32 [32768], P('col'), may hold values from -7 to 7
- window_roots: float32 [128], replicated, may hold values from 0 to 4, as said below
- deflated: int32 [32768], P('col'), may hold values 0 or 1
- column_map: int32 [32768], P('col'), may hold values from 0 to 32767, as said below
Outputs:
- vectors: float32 [2048, 128], P(('row', 'col'))
Inputs may be any that keep to these rules, and one draw needn't show every extreme that they name: `column_map`: A permutation of the 32768 columns. Grid column c holds columns c * 1024 to (c + 1) * 1024 - 1 and 16384 + c * 1024 to 16384 + (c + 1) * 1024 - 1 of the slab, and positions c * 2048 to (c + 1) * 2048 - 1. Of one grid column's positions, exactly 256 map to the columns of one grid column, 128 to each of 14 others, none to the remaining one. `secular_poles`: each pole lies between (k + 0.2) * 4 / 64 and (k + 0.8) * 4 / 64 for a whole number k. `window_roots`: each root lies within 0.15 * 4 / 64 of k * 4 / 64 for a whole number k of 1 to 63.
All inputs are finite; a program needn't handle non-finite values. No bound on the sum of `deflated` on one device may be relied on, other than what follows from the above.
Results may differ from a plain program's by a relative error of at most 0.0003.
Values sent between devices are 32-bit elements; how exact they have to be, the bound alone decides.
No kernel may reach another device: no remote copies, remote signals or barrier semaphores. Data moves between devices by JAX's collectives and lax.ppermute only.
A program may use at most 64 MiB of HBM per device.

v0:
```python
import jax
import jax.numpy as jnp
from jax import lax
from jax.sharding import PartitionSpec as P


def slot_plan(column_map, groups, cols_dev, capacity):
    block_len = column_map.shape[0]
    half_order = cols_dev * groups
    within = column_map % half_order
    target = within // cols_dev
    target_local = within % cols_dev + jnp.where(column_map >= half_order, cols_dev, 0)
    onehot = (target[:, None] == jnp.arange(groups, dtype=jnp.int32)[None, :]).astype(jnp.int32)
    slot_rank = jnp.sum(jnp.cumsum(onehot, axis=0) * onehot, axis=1) - 1
    slot_index = target * capacity + slot_rank
    sentinel = jnp.full((groups * capacity,), block_len, jnp.int32)
    slot_source = sentinel.at[slot_index].set(jnp.arange(block_len, dtype=jnp.int32))
    slot_target = sentinel.at[slot_index].set(target_local)
    return (slot_source, slot_target)


def route_generators(
    coupling, secular_poles, deflated, column_map, chosen_roots, inverse, groups, cols_dev, capacity
):
    block_len = column_map.shape[0]
    slot_source, slot_target = slot_plan(column_map, groups, cols_dev, capacity)
    live_coupling = jnp.where(deflated == 0, coupling, jnp.zeros_like(coupling))
    out_coupling = jnp.take(live_coupling, slot_source, mode="fill", fill_value=0.0).reshape(
        groups, capacity
    )
    out_poles = jnp.take(secular_poles, slot_source, mode="fill", fill_value=0.0).reshape(
        groups, capacity
    )
    got_coupling, got_poles, got_index = (
        lax.all_to_all(out_coupling, "col", split_axis=0, concat_axis=0, tiled=True),
        lax.all_to_all(out_poles, "col", split_axis=0, concat_axis=0, tiled=True),
        lax.all_to_all(
            slot_target.reshape(groups, capacity), "col", split_axis=0, concat_axis=0, tiled=True
        ),
    )
    distance = got_poles.reshape(-1)[:, None] - chosen_roots[None, :]
    rebuilt = got_coupling.reshape(-1)[:, None] / distance * inverse[None, :]
    empty = jnp.zeros((block_len, chosen_roots.shape[0]), jnp.float32)
    return empty.at[got_index.reshape(-1)].set(rebuilt, mode="drop")


def body(eigen_slab, secular_poles, coupling, window_roots, deflated, column_map):
    groups = lax.axis_size("col")
    row_groups = lax.axis_size("row")
    block_len = secular_poles.shape[0]
    cols_dev = eigen_slab.shape[1]
    capacity = 2 * (block_len // groups)
    distance = secular_poles[:, None] - window_roots[None, :]
    entries = jnp.where(
        deflated[:, None] == 0, coupling[:, None] / distance, jnp.zeros_like(distance)
    )
    sum_squares = lax.psum(jnp.sum(entries * entries, axis=0), "col")
    inverse = lax.rsqrt(sum_squares)
    placed = route_generators(
        coupling,
        secular_poles,
        deflated,
        column_map,
        window_roots,
        inverse,
        groups,
        cols_dev,
        capacity,
    )
    half_start = jnp.where(lax.axis_index("row") < row_groups // 2, 0, cols_dev)
    half_window = lax.dynamic_slice_in_dim(placed, half_start, cols_dev, 0)
    return lax.psum_scatter(
        jnp.dot(
            eigen_slab,
            half_window,
            precision=lax.Precision.HIGHEST,
            preferred_element_type=jnp.float32,
        ),
        "col",
        scatter_dimension=0,
        tiled=True,
    )


def solution(mesh):
    return jax.shard_map(
        body,
        mesh=mesh,
        in_specs=(P("row", "col"), P("col"), P("col"), P(), P("col"), P("col")),
        out_specs=P(("row", "col"), None),
        check_vma=False,
    )
```

profile of v0, /device:TPU:0, one launch (start us, length us, event | category | flops | bytes accessed | tf_op | source)
XLA Modules:
  0.0 217.3 jit_solution(6445857893102365710)
XLA Ops:
  6.5 0.7 fusion.15
  7.3 4.5 %reduce-window.6 = s32[16,16,128]{2,1,0:T(8,128)S(1)} reduce-window(s32[16,16,128]{2,1,0:T(8,128)S(1)} %fusion.12, s32[]{:T(128)} %constant.67.clone.1), window={size=1x1x128 pad=0_0x0_0x127_0}, to_apply=%region_0.1 | reduce-window | flops 4161536 | bytes 262148 | tf_op jit(solution)/shard_map/reduce-window
  11.8 0.4 slice_reduce_fusion
  12.3 0.2 reduce-window.9
  12.4 0.1 broadcast_add_fusion
  12.5 0.1 fusion.11
  12.6 8.6 %scatter_custom_fusion = s32[4096]{0:T(1024)} fusion(s32[2048]{0:T(1024)S(1)} %compare_select_fusion.2, s32[2048]{0:T(1024)S(1)} %get-tuple-element.10, s32[]{:T(128)} %constant.66.clone.1), kind=kCustom, calls=%fused_computation.45 | custom fusion | bytes 16388 | tf_op jit(solution)/shard_map/scatter | solution.py:18
  21.2 7.4 %all-to-all-start = ((s32[16,1,256]{2,1,0:T(1,128)}), s32[16,1,256]{2,1,0:T(1,128)S(1)}, u32[]{:S(2)}, u32[]{:S(2)}) async-start(s32[16,1,256]{2,1,0:T(1,128)} %bitcast.2), calls=%async_computation | async-start | bytes 32768 | tf_op jit(solution)/shard_map/all_to_all | solution.py:37
  28.6 8.1 %scatter_custom_fusion.1 = s32[4096]{0:T(1024)S(1)} fusion(s32[2048]{0:T(1024)S(1)} %compare_select_fusion.2, s32[2048]{0:T(1024)S(1)} %iota.11, s32[]{:T(128)} %constant.66.clone.1), kind=kCustom, calls=%fused_computation.43 | custom fusion | bytes 16388 | tf_op jit(solution)/shard_map/scatter | solution.py:17
  36.7 0.7 broadcast_select_fusion.2
  37.4 23.0 %gather_fusion = f32[4096]{0:T(1024)S(1)} fusion(f32[2048]{0:T(1024)S(1)} %get-tuple-element.8, s32[4096]{0:T(1024)S(1)} %fusion.13), kind=kCustom, calls=%fused_computation.clone | custom fusion | bytes 49152 | tf_op jit(solution)/shard_map/jit(_take)/gather | solution.py:28
  60.5 0.6 broadcast_select_fusion.1
  61.1 0.1 copy-done
  61.2 23.0 %gather_fusion.1 = f32[4096]{0:T(1024)S(1)} fusion(f32[2048]{0:T(1024)S(1)} %copy-done, s32[4096]{0:T(1024)S(1)} %fusion.13), kind=kCustom, calls=%fused_computation.1.clone | custom fusion | bytes 49152 | tf_op jit(solution)/shard_map/jit(_take)/gather | solution.py:31
  84.2 0.6 broadcast_select_fusion
  84.8 6.0 %all-to-all-start.2 = ((f32[16,1,256]{2,1,0:T(1,128)}), f32[16,1,256]{2,1,0:T(1,128)S(1)}, u32[]{:S(2)}, u32[]{:S(2)}) async-start(f32[16,1,256]{2,1,0:T(1,128)} %bitcast.7), calls=%async_computation.2 | async-start | bytes 32768 | tf_op jit(solution)/shard_map/all_to_all | solution.py:36
  90.9 1.0 multiply_reduce_fusion
  91.9 33.8 %psum.7 = f32[128]{0:T(128)S(1)} all-reduce(f32[128]{0:T(128)S(1)} %multiply_reduce_fusion), channel_id=1, replica_groups=mesh['row'=2,'col'=16] {'col'}, use_global_device_ids=true, to_apply=%region_6.8 | all-reduce | flops 128 | bytes 1024 | tf_op jit(solution)/shard_map/psum | solution.py:57
  125.7 3.5 %all-to-all-start.1 = ((f32[16,1,256]{2,1,0:T(1,128)}), f32[16,1,256]{2,1,0:T(1,128)S(1)}, u32[]{:S(2)}, u32[]{:S(2)}) async-start(f32[16,1,256]{2,1,0:T(1,128)} %bitcast.5), calls=%async_computation.1 | async-start | bytes 32768 | tf_op jit(solution)/shard_map/all_to_all | solution.py:35
  129.3 6.4 %all-to-all-done.1 = f32[16,1,256]{2,1,0:T(1,128)S(1)} async-done(((f32[16,1,256]{2,1,0:T(1,128)}), f32[16,1,256]{2,1,0:T(1,128)S(1)}, u32[]{:S(2)}, u32[]{:S(2)}) %all-to-all-start.1) | async-done | bytes 16416 | tf_op jit(solution)/shard_map/all_to_all | solution.py:35
  135.7 13.5 %scatter_custom_fusion.2 = f32[2048,128]{1,0:T(8,128)S(1)} fusion(s32[4096]{0:T(1024)S(1)} %bitcast.35, f32[128]{0:T(128)S(1)} %rsqrt.3, f32[128]{0:T(128)S(1)} %copy-done.2, f32[4096]{0:T(1024)S(1)} %bitcast.31, f32[4096]{0:T(1024)S(1)} %bitcast.32, f32[]{:T(128)} %constant.65.clone.1), kind=kCustom, calls=%fused_computation.5 | custom fusion | flops 1572864 | bytes 1082372 | tf_op jit(solution)/shard_map/scatter | solution.py:44
  149.2 6.7 %convolution_bitcast_fusion = f32[1024,128]{0,1:T(8,128)S(1)} fusion(f32[1024,1024]{1,0:T(8,128)} %param.8, f32[2048,128]{1,0:T(8,128)S(1)} %scatter_custom_fusion.2, s32[]{:T(128)S(6)} %select_n.62), kind=kOutput, calls=%fused_computation.9 | convolution fusion | flops 1610612736 | bytes 5242884 | tf_op jit(solution)/shard_map/dot_general | solution.py:73
  155.9 1.0 copy.11
  156.9 53.6 %reduce-scatter.4.cloned.1.call-done = f32[64,128]{1,0:T(8,128)} async-done(((f32[1024,128]{1,0:T(8,128)}), f32[64,128]{1,0:T(8,128)}) %reduce-scatter.4.cloned.1.call-update) | async-done | bytes 32784 | tf_op jit(solution)/shard_map/reduce_scatter | solution.py:72
  (15 shorter events, 0.1 us)
Async XLA Ops:
  21.2 63.6 %all-to-all-start = ((s32[16,1,256]{2,1,0:T(1,128)}), s32[16,1,256]{2,1,0:T(1,128)S(1)}, u32[]{:S(2)}, u32[]{:S(2)}) async-start(s32[16,1,256]{2,1,0:T(1,128)} %bitcast.2), calls=%async_computation | async-start | bytes 32768 | tf_op jit(solution)/shard_map/all_to_all | solution.py:37
  60.5 0.7 copy-start
  61.2 29.7 %copy-start.1 = (f32[2048]{0:T(1024)S(1)}, f32[2048]{0:T(1024)}, u32[]{:S(2)}) copy-start(f32[2048]{0:T(1024)} %param.10) | copy-start | bytes 24580
  61.2 29.7 %copy-start.2 = (f32[128]{0:T(128)S(1)}, f32[128]{0:T(128)}, u32[]{:S(2)}) copy-start(f32[128]{0:T(128)} %param.11) | copy-start | bytes 1540
  84.8 40.9 %all-to-all-start.2 = ((f32[16,1,256]{2,1,0:T(1,128)}), f32[16,1,256]{2,1,0:T(1,128)S(1)}, u32[]{:S(2)}, u32[]{:S(2)}) async-start(f32[16,1,256]{2,1,0:T(1,128)} %bitcast.7), calls=%async_computation.2 | async-start | bytes 32768 | tf_op jit(solution)/shard_map/all_to_all | solution.py:36
  125.7 10.0 %all-to-all-start.1 = ((f32[16,1,256]{2,1,0:T(1,128)}), f32[16,1,256]{2,1,0:T(1,128)S(1)}, u32[]{:S(2)}, u32[]{:S(2)}) async-start(f32[16,1,256]{2,1,0:T(1,128)} %bitcast.5), calls=%async_computation.1 | async-start | bytes 32768 | tf_op jit(solution)/shard_map/all_to_all | solution.py:35
  129.2 81.3 %reduce-scatter.4.cloned.1.call-start = ((), (), s32[]{:S(2)}) async-start(), calls=%async_computation.4 | async-start | bytes 557056 | tf_op jit(solution)/shard_map/reduce_scatter | solution.py:72
Sparse Core Ops, SparseCore 0:
  157.0 53.4 reduce-scatter.3
where the time goes:
time: 218 us; the launch traced here: 217 us
  local copies, waits for them, and re-layouts  64.3 us (29%)
  waiting for transfers between devices  60 us (28%)
  blocking collectives  33.8 us (16%)
  other arithmetic  22.1 us (10%)
  starting transfers between devices  16.9 us (8%)
  between operations  13.6 us (6%)
  matrix products  6.67 us (3%)
    reduce_scatter x1, waiting for transfers between devices, body(): lax.psum_scatter(jnp.dot(eigen_slab, half_window, precision=lax.Precision...  53.6 us
    psum x1, blocking collectives, body(): sum_squares = lax.psum(jnp.sum(entries * entries, axis=0), 'col')  33.8 us
    gather x1, local copies, waits for them, and re-layouts, route_generators(): jnp.take(live_coupling, slot_source, mode='fill', fill_value=0.0)  23 us
    gather x1, local copies, waits for them, and re-layouts, route_generators(): jnp.take(secular_poles, slot_source, mode='fill', fill_value=0.0)  23 us
    scatter x1, other arithmetic, route_generators(): return empty.at[got_index.reshape(-1)].set(rebuilt, mode='drop')  13.5 us
    scatter x1, local copies, waits for them, and re-layouts, slot_plan(): slot_target = sentinel.at[slot_index].set(target_local)  8.62 us
    scatter x1, local copies, waits for them, and re-layouts, slot_plan(): sentinel.at[slot_index].set(jnp.arange(block_len, dtype=jnp.int32))  8.06 us
    all_to_all x1, starting transfers between devices, route_generators(): lax.all_to_all(slot_target.reshape(groups, capacity), 'col', split_axis=0...  7.39 us
  transfers between devices with their start and end apart: 4, of which 2 were waited for; matrix products, arithmetic and copies ran while one was open for 26% of the time, Pallas kernels for 0%

commit v1 on v0

--- a/solution.py
+++ b/solution.py
@@ -54,7 +54,7 @@
     entries = jnp.where(
         deflated[:, None] == 0, coupling[:, None] / distance, jnp.zeros_like(distance)
     )
-    sum_squares = lax.psum(jnp.sum(entries * entries, axis=0), "col")
+    sum_squares = jnp.sum(lax.all_gather(jnp.sum(entries * entries, axis=0), "col"), axis=0)
     inverse = lax.rsqrt(sum_squares)
     placed = route_generators(
         coupling,

time: 218 us -> 206 us (0.945)
  blocking collectives: 33.8 us -> 21.7 us
    psum x1 -> x0, blocking collectives: 33.8 us -> none  [body(): sum_squares = lax.psum(jnp.sum(entries * entries, axis=0), 'col')]
    all_gather x0 -> x1, blocking collectives: none -> 21.7 us  [body(): lax.all_gather(jnp.sum(entries * entries, axis=0), 'col')]
  transfers between devices with their start and end apart: 4 -> 4, of which waited for: 2 -> 2; matrix products, arithmetic and copies ran while one was open for 26% -> 28% of each run, Pallas kernels for 0% -> 0%
where the time goes in v1:
time: 206 us; the launch traced here: 205 us
  local copies, waits for them, and re-layouts  64.3 us (31%)
  waiting for transfers between devices  59.9 us (29%)
  other arithmetic  22.1 us (11%)
  blocking collectives  21.7 us (11%)
  starting transfers between devices  16.9 us (8%)
  between operations  13.6 us (7%)
  matrix products  6.67 us (3%)
    reduce_scatter x1, waiting for transfers between devices, body(): lax.psum_scatter(jnp.dot(eigen_slab, half_window, precision=lax.Precision...  53.5 us
    gather x1, local copies, waits for them, and re-layouts, route_generators(): jnp.take(live_coupling, slot_source, mode='fill', fill_value=0.0)  23 us
    gather x1, local copies, waits for them, and re-layouts, route_generators(): jnp.take(secular_poles, slot_source, mode='fill', fill_value=0.0)  23 us
    all_gather x1, blocking collectives, body(): lax.all_gather(jnp.sum(entries * entries, axis=0), 'col')  21.7 us
    scatter x1, other arithmetic, route_generators(): return empty.at[got_index.reshape(-1)].set(rebuilt, mode='drop')  13.5 us
    scatter x1, local copies, waits for them, and re-layouts, slot_plan(): slot_target = sentinel.at[slot_index].set(target_local)  8.62 us
    scatter x1, local copies, waits for them, and re-layouts, slot_plan(): sentinel.at[slot_index].set(jnp.arange(block_len, dtype=jnp.int32))  8.06 us
    all_to_all x1, starting transfers between devices, route_generators(): lax.all_to_all(slot_target.reshape(groups, capacity), 'col', split_axis=0...  7.39 us
  transfers between devices with their start and end apart: 4, of which 2 were waited for; matrix products, arithmetic and copies ran while one was open for 28% of the time, Pallas kernels for 0%

profile of v1, /device:TPU:0, one launch (start us, length us, event | category | flops | bytes accessed | tf_op | source)
XLA Modules:
  0.0 205.2 jit_solution(10435111361272829224)
XLA Ops:
  6.5 0.7 fusion.15
  7.3 4.5 %reduce-window.6 = s32[16,16,128]{2,1,0:T(8,128)S(1)} reduce-window(s32[16,16,128]{2,1,0:T(8,128)S(1)} %fusion.12, s32[]{:T(128)} %constant.67.clone.1), window={size=1x1x128 pad=0_0x0_0x127_0}, to_apply=%region_0.1 | reduce-window | flops 4161536 | bytes 262148 | tf_op jit(solution)/shard_map/reduce-window
  11.8 0.4 slice_reduce_fusion
  12.3 0.2 reduce-window.9
  12.4 0.1 broadcast_add_fusion
  12.5 0.1 fusion.11
  12.6 8.6 %scatter_custom_fusion = s32[4096]{0:T(1024)} fusion(s32[2048]{0:T(1024)S(1)} %compare_select_fusion.2, s32[2048]{0:T(1024)S(1)} %get-tuple-element.10, s32[]{:T(128)} %constant.66.clone.1), kind=kCustom, calls=%fused_computation.45 | custom fusion | bytes 16388 | tf_op jit(solution)/shard_map/scatter | solution.py:18
  21.2 7.4 %all-to-all-start = ((s32[16,1,256]{2,1,0:T(1,128)}), s32[16,1,256]{2,1,0:T(1,128)S(1)}, u32[]{:S(2)}, u32[]{:S(2)}) async-start(s32[16,1,256]{2,1,0:T(1,128)} %bitcast.2), calls=%async_computation | async-start | bytes 32768 | tf_op jit(solution)/shard_map/all_to_all | solution.py:37
  28.6 8.1 %scatter_custom_fusion.1 = s32[4096]{0:T(1024)S(1)} fusion(s32[2048]{0:T(1024)S(1)} %compare_select_fusion.2, s32[2048]{0:T(1024)S(1)} %iota.11, s32[]{:T(128)} %constant.66.clone.1), kind=kCustom, calls=%fused_computation.43 | custom fusion | bytes 16388 | tf_op jit(solution)/shard_map/scatter | solution.py:17
  36.7 0.7 broadcast_select_fusion.2
  37.4 23.0 %gather_fusion = f32[4096]{0:T(1024)S(1)} fusion(f32[2048]{0:T(1024)S(1)} %get-tuple-element.8, s32[4096]{0:T(1024)S(1)} %fusion.13), kind=kCustom, calls=%fused_computation.clone | custom fusion | bytes 49152 | tf_op jit(solution)/shard_map/jit(_take)/gather | solution.py:28
  60.5 0.6 broadcast_select_fusion.1
  61.1 0.1 copy-done
  61.2 23.0 %gather_fusion.1 = f32[4096]{0:T(1024)S(1)} fusion(f32[2048]{0:T(1024)S(1)} %copy-done, s32[4096]{0:T(1024)S(1)} %fusion.13), kind=kCustom, calls=%fused_computation.1.clone | custom fusion | bytes 49152 | tf_op jit(solution)/shard_map/jit(_take)/gather | solution.py:31
  84.2 0.6 broadcast_select_fusion
  84.8 6.0 %all-to-all-start.2 = ((f32[16,1,256]{2,1,0:T(1,128)}), f32[16,1,256]{2,1,0:T(1,128)S(1)}, u32[]{:S(2)}, u32[]{:S(2)}) async-start(f32[16,1,256]{2,1,0:T(1,128)} %bitcast.7), calls=%async_computation.2 | async-start | bytes 32768 | tf_op jit(solution)/shard_map/all_to_all | solution.py:36
  90.9 1.0 multiply_reduce_fusion
  91.9 21.7 %all-gather.1 = f32[16,1,128]{2,1,0:T(1,128)S(1)} all-gather(f32[1,1,128]{2,1,0:T(1,128)S(1)} %bitcast.37), channel_id=2, replica_groups=mesh['row'=2,'col'=16] {'col'}, dimensions={0}, use_global_device_ids=true | all-gather | bytes 8704 | tf_op jit(solution)/shard_map/all_gather | solution.py:57
  113.6 3.5 %all-to-all-start.1 = ((f32[16,1,256]{2,1,0:T(1,128)}), f32[16,1,256]{2,1,0:T(1,128)S(1)}, u32[]{:S(2)}, u32[]{:S(2)}) async-start(f32[16,1,256]{2,1,0:T(1,128)} %bitcast.5), calls=%async_computation.1 | async-start | bytes 32768 | tf_op jit(solution)/shard_map/all_to_all | solution.py:35
  117.2 6.4 %all-to-all-done.1 = f32[16,1,256]{2,1,0:T(1,128)S(1)} async-done(((f32[16,1,256]{2,1,0:T(1,128)}), f32[16,1,256]{2,1,0:T(1,128)S(1)}, u32[]{:S(2)}, u32[]{:S(2)}) %all-to-all-start.1) | async-done | bytes 16416 | tf_op jit(solution)/shard_map/all_to_all | solution.py:35
  123.6 13.5 %scatter_custom_fusion.2 = f32[2048,128]{1,0:T(8,128)S(1)} fusion(s32[4096]{0:T(1024)S(1)} %bitcast.36, f32[128]{0:T(128)S(1)} %rsqrt.7, f32[128]{0:T(128)S(1)} %copy-done.2, f32[4096]{0:T(1024)S(1)} %bitcast.32, f32[4096]{0:T(1024)S(1)} %bitcast.33, f32[]{:T(128)} %constant.65.clone.1), kind=kCustom, calls=%fused_computation.5 | custom fusion | flops 1572864 | bytes 1082372 | tf_op jit(solution)/shard_map/scatter | solution.py:44
  137.1 6.7 %convolution_bitcast_fusion = f32[1024,128]{0,1:T(8,128)S(1)} fusion(f32[1024,1024]{1,0:T(8,128)} %param.8, f32[2048,128]{1,0:T(8,128)S(1)} %scatter_custom_fusion.2, s32[]{:T(128)S(6)} %select_n.62), kind=kOutput, calls=%fused_computation.9 | convolution fusion | flops 1610612736 | bytes 5242884 | tf_op jit(solution)/shard_map/dot_general | solution.py:73
  143.8 1.0 copy.11
  144.8 53.5 %reduce-scatter.4.cloned.1.call-done = f32[64,128]{1,0:T(8,128)} async-done(((f32[1024,128]{1,0:T(8,128)}), f32[64,128]{1,0:T(8,128)}) %reduce-scatter.4.cloned.1.call-update) | async-done | bytes 32784 | tf_op jit(solution)/shard_map/reduce_scatter | solution.py:72
  (16 shorter events, 0.2 us)
Async XLA Ops:
  21.2 63.6 %all-to-all-start = ((s32[16,1,256]{2,1,0:T(1,128)}), s32[16,1,256]{2,1,0:T(1,128)S(1)}, u32[]{:S(2)}, u32[]{:S(2)}) async-start(s32[16,1,256]{2,1,0:T(1,128)} %bitcast.2), calls=%async_computation | async-start | bytes 32768 | tf_op jit(solution)/shard_map/all_to_all | solution.py:37
  60.5 0.7 copy-start
  61.2 29.7 %copy-start.1 = (f32[2048]{0:T(1024)S(1)}, f32[2048]{0:T(1024)}, u32[]{:S(2)}) copy-start(f32[2048]{0:T(1024)} %param.10) | copy-start | bytes 24580
  61.2 29.7 %copy-start.2 = (f32[128]{0:T(128)S(1)}, f32[128]{0:T(128)}, u32[]{:S(2)}) copy-start(f32[128]{0:T(128)} %param.11) | copy-start | bytes 1540
  84.8 28.8 %all-to-all-start.2 = ((f32[16,1,256]{2,1,0:T(1,128)}), f32[16,1,256]{2,1,0:T(1,128)S(1)}, u32[]{:S(2)}, u32[]{:S(2)}) async-start(f32[16,1,256]{2,1,0:T(1,128)} %bitcast.7), calls=%async_computation.2 | async-start | bytes 32768 | tf_op jit(solution)/shard_map/all_to_all | solution.py:36
  113.6 10.0 %all-to-all-start.1 = ((f32[16,1,256]{2,1,0:T(1,128)}), f32[16,1,256]{2,1,0:T(1,128)S(1)}, u32[]{:S(2)}, u32[]{:S(2)}) async-start(f32[16,1,256]{2,1,0:T(1,128)} %bitcast.5), calls=%async_computation.1 | async-start | bytes 32768 | tf_op jit(solution)/shard_map/all_to_all | solution.py:35
  117.1 81.2 %reduce-scatter.4.cloned.1.call-start = ((), (), s32[]{:S(2)}) async-start(), calls=%async_computation.4 | async-start | bytes 557056 | tf_op jit(solution)/shard_map/reduce_scatter | solution.py:72
Sparse Core Ops, SparseCore 0:
  145.0 53.3 reduce-scatter.3
